TPU v7x, 128 devices: a whole 4x4x4 slice. The times are simulated.
128 devices in a mesh: wide: 8 (over z_hi, y), narrow: 16 (over x, z_lo, core).
Axes of the slice: x: 4, y: 4, z: 4 (z_hi: 2, z_lo: 2; z = z_hi * 2 + z_lo), core: 2. Of those that a mesh axis runs over, the one named last changes fastest.
Arguments:
- hinv_start: float32 [16384, 16384], P('wide', 'narrow'), as said below
- weights: bfloat16 [2048, 16384], P('narrow', 'wide'), may hold values from -6 to 6
- removed: int32 [1, 512], replicated, may hold values from 0 to 16383, as said below
Outputs:
- hinv_out: float32 [16384, 16384], P('wide', 'narrow')
- weights_out: bfloat16 [2048, 16384], P('narrow', 'wide')
Inputs may be any that keep to these rules, and one draw needn't show every extreme that they name: `removed`: all 1 x 512 indices are distinct; 0 and 16383 are always among them. `hinv_start`: symmetric and positive definite.
All inputs are finite; a program needn't handle non-finite values. Where the computation divides by a largest or mean magnitude, that divisor is 1e-20 or more.
Results may differ from a plain program's by a relative error of at most 0.0036.
Values may be sent and summed in bfloat16 or wider, within the bound.
No kernel may reach another device: no remote copies, remote signals or barrier semaphores. Data moves between devices by JAX's collectives and lax.ppermute only.
A program may use at most 128 MiB of HBM per device.

v0:
```python
import jax
import jax.numpy as jnp
from jax import lax
from jax.sharding import PartitionSpec as P

ITERS = 8


def from_root(x, axis, root):
    mine = lax.axis_index(axis) == root
    return lax.psum(jnp.where(mine, x, jnp.zeros_like(x)), axis)


def per_device(hinv_start, weights, removed):
    wide_count = lax.axis_size("wide")
    narrow_count = lax.axis_size("narrow")
    row_count, col_count = hinv_start.shape
    row_start = lax.axis_index("wide") * row_count
    col_start = lax.axis_index("narrow") * col_count
    blocks_each = narrow_count // wide_count
    block = removed.shape[1]
    identity = jnp.eye(block, dtype=jnp.float32)
    hess = hinv_start
    wmat = weights
    column_ids = row_start + jnp.arange(row_count, dtype=jnp.int32)
    picked = removed[0]
    row_hit = (picked >= row_start) & (picked < row_start + row_count)
    row_local = jnp.clip(picked - row_start, 0, row_count - 1)
    col_hit = (picked >= col_start) & (picked < col_start + col_count)
    col_local = jnp.clip(picked - col_start, 0, col_count - 1)
    row_part = jnp.where(row_hit[:, None], jnp.take(hess, row_local, axis=0), 0.0)
    weight_part = jnp.where(
        row_hit[None, :], jnp.take(wmat, row_local, axis=1).astype(jnp.float32), 0.0
    )
    rows_here, chosen = lax.psum((row_part, weight_part), "wide")
    pivot_part = jnp.where(col_hit[None, :], jnp.take(rows_here, col_local, axis=1), 0.0)
    pivot = lax.psum(pivot_part, "narrow")
    first_root = lax.axis_index("wide") * blocks_each
    col_part = jnp.where(col_hit[None, :], jnp.take(hess, col_local, axis=1), 0.0)
    columns = lax.psum(col_part, "narrow")
    rounded = rows_here.astype(jnp.bfloat16)
    pieces = []
    for offset in range(blocks_each):
        pieces.append(from_root(rounded, "narrow", first_root + offset))
    panel = jnp.concatenate(pieces, axis=1)
    scale = 1.0 / jnp.max(jnp.sum(jnp.abs(pivot), axis=1))
    start_guess = identity * scale
    width = block // wide_count
    own = lax.axis_index("wide") * width
    eye_cols = lax.dynamic_slice_in_dim(identity, own, width, 1)
    current = lax.dynamic_slice_in_dim(start_guess, own, width, 1)
    for turn in range(ITERS):
        right = 2.0 * eye_cols - jnp.dot(pivot, current, precision=lax.Precision.HIGHEST)

        def add_wide(total, piece, start, right=right):
            return jnp.dot(piece, right, precision=lax.Precision.HIGHEST)

        current = add_wide(
            jnp.zeros((block, width), jnp.float32),
            lax.all_gather(current, "wide", axis=1, tiled=True),
            jnp.int32(0),
        )
    inverse = lax.all_gather(current, "wide", axis=1, tiled=True)
    gain = jnp.dot(chosen, inverse, precision=lax.Precision.HIGHEST).astype(jnp.bfloat16)
    delta = jnp.dot(gain, panel, preferred_element_type=jnp.float32)
    cleared = jnp.any(picked[:, None] == column_ids[None, :], axis=0)
    wmat = jnp.where(cleared[None, :], 0.0, wmat.astype(jnp.float32) - delta).astype(jnp.bfloat16)
    inner_rows = jnp.dot(inverse, rows_here, precision=lax.Precision.HIGHEST)
    hess = hess - jnp.dot(columns, inner_rows, precision=lax.Precision.HIGHEST)
    return (hess, wmat)


def solution(mesh):
    return jax.shard_map(
        per_device,
        mesh=mesh,
        in_specs=(P("wide", "narrow"), P("narrow", "wide"), P()),
        out_specs=(P("wide", "narrow"), P("narrow", "wide")),
        check_vma=False,
    )
```

profile of v0, /device:TPU:0, one launch (start us, length us, event | category | flops | bytes accessed | tf_op | source)
XLA Modules:
  0.0 836.1 jit_solution(4168252360116877082)
XLA Ops:
  12.0 6.2 gather_fusion.1
  20.9 9.1 %copy.15 = f32[2048,1024]{0,1:T(8,128)} copy(f32[2048,1024]{1,0:T(8,128)} %param.3) | data formatting | bytes 16777216 | tf_op args[0]
  30.0 9.0 %gather_fusion = f32[512,2048]{1,0:T(8,128)} fusion(f32[2048,1024]{0,1:T(8,128)} %copy.15, s32[1024]{0:T(1024)S(1)} %pad_clamp_fusion.1), kind=kCustom, calls=%fused_computation | custom fusion | bytes 8390656 | tf_op jit(solution)/shard_map/jit(_take)/gather | solution.py:39
  39.0 4.7 select_bitcast_fusion
  43.7 73.7 %all-reduce.9.cloned.1.call-done = (f32[512,1024]{1,0:T(8,128)}, f32[128,512]{0,1:T(8,128)}) async-done(((f32[512,1024]{1,0:T(8,128)}, f32[128,512]{0,1:T(8,128)}), (f32[512,1024]{1,0:T(8,128)}, f32[128,512]{0,1:T(8,128)})) %all-reduce.9.cloned.1.call-update) | async-done | bytes 2359312 | tf_op jit(solution)/shard_map/psum | solution.py:35
  122.7 135.8 %all-reduce.7.cloned.1.call-done = (f32[2048,512]{0,1:T(8,128)}, f32[512,512]{1,0:T(8,128)}) async-done(((f32[2048,512]{0,1:T(8,128)}, f32[512,512]{1,0:T(8,128)}), (f32[2048,512]{0,1:T(8,128)}, f32[512,512]{1,0:T(8,128)})) %all-reduce.7.cloned.1.call-update) | async-done | bytes 5242896 | tf_op jit(solution)/shard_map/psum | solution.py:40
  264.4 45.5 %all-gather.10.cloned.1.call-done = f32[512,512]{0,1:T(8,128)} async-done(((f32[512,64]{0,1:T(8,128)}), f32[512,512]{0,1:T(8,128)}) %all-gather.10.cloned.1.call-update) | async-done | bytes 1048592 | tf_op jit(solution)/shard_map/all_gather | solution.py:60
  314.7 44.0 %all-gather.12.cloned.1.call-done = f32[512,512]{0,1:T(8,128)} async-done(((f32[512,64]{0,1:T(8,128)}), f32[512,512]{0,1:T(8,128)}) %all-gather.12.cloned.1.call-update) | async-done | bytes 1048592 | tf_op jit(solution)/shard_map/all_gather | solution.py:60
  358.7 2.7 fusion.8
  363.5 44.0 %all-gather.14.cloned.1.call-done = f32[512,512]{0,1:T(8,128)} async-done(((f32[512,64]{0,1:T(8,128)}), f32[512,512]{0,1:T(8,128)}) %all-gather.14.cloned.1.call-update) | async-done | bytes 1048592 | tf_op jit(solution)/shard_map/all_gather | solution.py:60
  407.5 2.7 fusion.9
  412.5 43.8 %all-gather.16.cloned.1.call-done = f32[512,512]{0,1:T(8,128)} async-done(((f32[512,64]{0,1:T(8,128)}), f32[512,512]{0,1:T(8,128)}) %all-gather.16.cloned.1.call-update) | async-done | bytes 1048592 | tf_op jit(solution)/shard_map/all_gather | solution.py:60
  456.3 2.7 fusion.10
  461.1 44.1 %all-gather.18.cloned.1.call-done = f32[512,512]{0,1:T(8,128)} async-done(((f32[512,64]{0,1:T(8,128)}), f32[512,512]{0,1:T(8,128)}) %all-gather.18.cloned.1.call-update) | async-done | bytes 1048592 | tf_op jit(solution)/shard_map/all_gather | solution.py:60
  510.1 43.9 %all-gather.20.cloned.1.call-done = f32[512,512]{0,1:T(8,128)} async-done(((f32[512,64]{0,1:T(8,128)}), f32[512,512]{0,1:T(8,128)}) %all-gather.20.cloned.1.call-update) | async-done | bytes 1048592 | tf_op jit(solution)/shard_map/all_gather | solution.py:60
  558.8 44.1 %all-gather.22.cloned.1.call-done = f32[512,512]{0,1:T(8,128)} async-done(((f32[512,64]{0,1:T(8,128)}), f32[512,512]{0,1:T(8,128)}) %all-gather.22.cloned.1.call-update) | async-done | bytes 1048592 | tf_op jit(solution)/shard_map/all_gather | solution.py:60
  602.9 2.7 fusion.13
  607.8 44.0 %all-gather.24.cloned.1.call-done = f32[512,512]{0,1:T(8,128)} async-done(((f32[512,64]{0,1:T(8,128)}), f32[512,512]{0,1:T(8,128)}) %all-gather.24.cloned.1.call-update) | async-done | bytes 1048592 | tf_op jit(solution)/shard_map/all_gather | solution.py:60
  651.7 2.7 fusion.14
  657.0 43.7 %all-gather.26.cloned.1.call-done = f32[512,512]{0,1:T(8,128)} async-done(((f32[512,64]{0,1:T(8,128)}), f32[512,512]{0,1:T(8,128)}) %all-gather.26.cloned.1.call-update) | async-done | bytes 1048592 | tf_op jit(solution)/shard_map/all_gather | solution.py:63
  703.2 4.7 fusion.15
  708.0 17.1 %convolution_subtract_fusion = f32[2048,1024]{1,0:T(8,128)} fusion(f32[2048,1024]{1,0:T(8,128)} %param.3, f32[2048,512]{0,1:T(8,128)S(1)} %copy-done.2, f32[512,1024]{1,0:T(8,128)S(1)} %fusion.15), kind=kOutput, calls=%fused_computation.6 | convolution fusion | flops 12886999040 | bytes 23068672 | tf_op jit(solution)/shard_map/dot_general | solution.py:69
  725.0 101.4 %all-reduce.11.cloned.1.call-done = (bf16[512,1024]{1,0:T(8,128)(2,1)}, bf16[512,1024]{1,0:T(8,128)(2,1)}) async-done(((bf16[512,1024]{1,0:T(8,128)(2,1)}, bf16[512,1024]{1,0:T(8,128)(2,1)}), (bf16[512,1024]{1,0:T(8,128)(2,1)}, bf16[512,1024]{1,0:T(8,128)(2,1)})) %all-reduce.11.cloned.1.call-update) | async-done | bytes 2097168 | tf_op jit(solution)/shard_map/psum | solution.py:11
  826.4 2.8 fusion.1
  (68 shorter events, 46.1 us)
Async XLA Ops:
  7.2 110.3 %all-reduce.9.cloned.1.call-start = ((), (), s32[]{:S(2)}) async-start(), calls=%async_computation.10 | async-start | bytes 4718592 | tf_op jit(solution)/shard_map/psum | solution.py:35
  20.8 237.7 %all-reduce.7.cloned.1.call-start = ((), (), s32[]{:S(2)}) async-start(), calls=%async_computation.9 | async-start | bytes 10485760 | tf_op jit(solution)/shard_map/psum | solution.py:40
  122.6 187.4 %all-gather.10.cloned.1.call-start = ((), (), s32[]{:S(2)}) async-start(), calls=%async_computation | async-start | bytes 1179648 | tf_op jit(solution)/shard_map/all_gather | solution.py:60
  258.5 54.2 %copy-start = (f32[512,512]{1,0:T(8,128)S(1)}, f32[512,512]{1,0:T(8,128)}, u32[]{:S(2)}) copy-start(f32[512,512]{1,0:T(8,128)} %get-tuple-element.5) | copy-start | bytes 3145732
  262.0 96.7 %all-gather.12.cloned.1.call-start = ((), (), s32[]{:S(2)}) async-start(), calls=%async_computation.1 | async-start | bytes 1179648 | tf_op jit(solution)/shard_map/all_gather | solution.py:60
  312.6 94.9 %all-gather.14.cloned.1.call-start = ((), (), s32[]{:S(2)}) async-start(), calls=%async_computation.2 | async-start | bytes 1179648 | tf_op jit(solution)/shard_map/all_gather | solution.py:60
  361.4 94.9 %all-gather.16.cloned.1.call-start = ((), (), s32[]{:S(2)}) async-start(), calls=%async_computation.3 | async-start | bytes 1179648 | tf_op jit(solution)/shard_map/all_gather | solution.py:60
  410.2 95.0 %all-gather.18.cloned.1.call-start = ((), (), s32[]{:S(2)}) async-start(), calls=%async_computation.4 | async-start | bytes 1179648 | tf_op jit(solution)/shard_map/all_gather | solution.py:60
  459.0 95.1 %all-gather.20.cloned.1.call-start = ((), (), s32[]{:S(2)}) async-start(), calls=%async_computation.5 | async-start | bytes 1179648 | tf_op jit(solution)/shard_map/all_gather | solution.py:60
  507.9 146.8 %copy-start.1 = (f32[512,1024]{1,0:T(8,128)S(1)}, f32[512,1024]{1,0:T(8,128)}, u32[]{:S(2)}) copy-start(f32[512,1024]{1,0:T(8,128)} %get-tuple-element.6) | copy-start | bytes 6291460
  507.9 95.1 %all-gather.22.cloned.1.call-start = ((), (), s32[]{:S(2)}) async-start(), calls=%async_computation.6 | async-start | bytes 1179648 | tf_op jit(solution)/shard_map/all_gather | solution.py:60
  556.7 95.0 %all-gather.24.cloned.1.call-start = ((), (), s32[]{:S(2)}) async-start(), calls=%async_computation.7 | async-start | bytes 1179648 | tf_op jit(solution)/shard_map/all_gather | solution.py:60
  605.6 95.0 %all-gather.26.cloned.1.call-start = ((), (), s32[]{:S(2)}) async-start(), calls=%async_computation.8 | async-start | bytes 1179648 | tf_op jit(solution)/shard_map/all_gather | solution.py:63
  607.7 48.6 %copy-start.5 = (s32[1,512]{1,0:T(1,128)S(1)}, s32[1,512]{1,0:T(1,128)}, u32[]{:S(2)}) copy-start(s32[1,512]{1,0:T(1,128)} %param.5) | copy-start | bytes 6148
  607.7 92.9 %copy-start.4 = (f32[128,512]{0,1:T(8,128)S(1)}, f32[128,512]{0,1:T(8,128)}, u32[]{:S(2)}) copy-start(f32[128,512]{0,1:T(8,128)} %get-tuple-element.7) | copy-start | bytes 786436
  654.4 172.0 %all-reduce.11.cloned.1.call-start = ((), (), s32[]{:S(2)}) async-start(), calls=%async_computation.11 | async-start | bytes 4194304 | tf_op jit(solution)/shard_map/psum | solution.py:11
  700.6 7.3 copy-start.2
  708.0 118.4 %copy-start.3 = (bf16[128,2048]{1,0:T(8,128)(2,1)S(1)}, bf16[128,2048]{1,0:T(8,128)(2,1)}, u32[]{:S(2)}) copy-start(bf16[128,2048]{1,0:T(8,128)(2,1)} %param.4) | copy-start | bytes 1572868
Sparse Core Ops, SparseCore 0:
  21.0 96.4 all-reduce.8
  122.7 135.7 all-reduce.6
  262.1 47.7 all-gather.9
  312.7 45.9 all-gather.11
  361.5 45.9 all-gather.13
  410.3 45.9 all-gather.15
  459.2 45.9 all-gather.17
  508.1 45.9 all-gather.19
  557.0 45.9 all-gather.21
  605.8 45.9 all-gather.23
  654.6 45.9 all-gather.25
  703.0 123.3 all-reduce.10
where the time goes:
time: 837 us; the launch traced here: 836 us
  waiting for transfers between devices  708 us (85%)
  matrix products  65.4 us (8%)
  local copies, waits for them, and re-layouts  30.9 us (4%)
  other arithmetic  15.7 us (2%)
  between operations  15.1 us (2%)
    all_gather x8, waiting for transfers between devices, per_device(): lax.all_gather(current, 'wide', axis=1, tiled=True)  353 us
    psum x1, waiting for transfers between devices, per_device(): columns = lax.psum(col_part, 'narrow')  136 us
    psum x1, waiting for transfers between devices, from_root(): return lax.psum(jnp.where(mine, x, jnp.zeros_like(x)), axis)  101 us
    psum x1, waiting for transfers between devices, per_device(): rows_here, chosen = lax.psum((row_part, weight_part), 'wide')  73.7 us
    all_gather x1, waiting for transfers between devices, per_device(): inverse = lax.all_gather(current, 'wide', axis=1, tiled=True)  43.7 us
    dot_general x8, matrix products, add_wide(): return jnp.dot(piece, right, precision=lax.Precision.HIGHEST)  21.3 us
    dot_general x1, matrix products, per_device(): hess = hess - jnp.dot(columns, inner_rows, precision=lax.Precision.HIGHEST)  17.1 us
    dot_general x8, matrix products, per_device(): jnp.dot(pivot, current, precision=lax.Precision.HIGHEST)  16.9 us
  transfers between devices with their start and end apart: 12, of which 12 were waited for; matrix products, arithmetic and copies ran while one was open for 8% of the time, Pallas kernels for 0%

commit v1 on v0

--- a/solution.py
+++ b/solution.py
@@ -37,7 +37,7 @@
     pivot = lax.psum(pivot_part, "narrow")
     first_root = lax.axis_index("wide") * blocks_each
     col_part = jnp.where(col_hit[None, :], jnp.take(hess, col_local, axis=1), 0.0)
-    columns = lax.psum(col_part, "narrow")
+    columns = jnp.sum(lax.all_gather(col_part, "narrow"), axis=0)
     rounded = rows_here.astype(jnp.bfloat16)
     pieces = []
     for offset in range(blocks_each):

time: 837 us -> 1190 us (1.42)
  waiting for transfers between devices: 708 us -> 1030 us
  other arithmetic: 15.7 us -> 38.6 us
    all_gather x0 -> x1, waiting for transfers between devices: none -> 323 us  [per_device(): columns = jnp.sum(lax.all_gather(col_part, 'narrow'), axis=0)]
    all_gather x1, waiting for transfers between devices: 43.7 us -> 15.2 us  [per_device(): inverse = lax.all_gather(current, 'wide', axis=1, tiled=True)]
    unnamed x0 -> x1, other arithmetic: none -> 23.1 us
    psum x1, waiting for transfers between devices: 73.7 us -> 96.5 us  [per_device(): rows_here, chosen = lax.psum((row_part, weight_part), 'wide')]
    psum x1, waiting for transfers between devices: 101 us -> 123 us  [from_root(): return lax.psum(jnp.where(mine, x, jnp.zeros_like(x)), axis)]
    psum x1, waiting for transfers between devices: 136 us -> 118 us  [per_device(): pivot = lax.psum(pivot_part, 'narrow')]
  transfers between devices with their start and end apart: 12 -> 13, of which waited for: 12 -> 13; matrix products, arithmetic and copies ran while one was open for 8% -> 5% of each run, Pallas kernels for 0% -> 0%
where the time goes in v1:
time: 1190 us
  waiting for transfers between devices  1030 us (87%)
  matrix products  66.2 us (6%)
  other arithmetic  38.6 us (3%)
  local copies, waits for them, and re-layouts  36.7 us (3%)
  between operations  14.7 us (1%)
    all_gather x8, waiting for transfers between devices, per_device(): lax.all_gather(current, 'wide', axis=1, tiled=True)  354 us
    all_gather x1, waiting for transfers between devices, per_device(): columns = jnp.sum(lax.all_gather(col_part, 'narrow'), axis=0)  323 us
    psum x1, waiting for transfers between devices, from_root(): return lax.psum(jnp.where(mine, x, jnp.zeros_like(x)), axis)  123 us
    psum x1, waiting for transfers between devices, per_device(): pivot = lax.psum(pivot_part, 'narrow')  118 us
    psum x1, waiting for transfers between devices, per_device(): rows_here, chosen = lax.psum((row_part, weight_part), 'wide')  96.5 us
  transfers between devices with their start and end apart: 13, of which 13 were waited for; matrix products, arithmetic and copies ran while one was open for 5% of the time, Pallas kernels for 0%

profile of v1, /device:TPU:0, one launch (start us, length us, event | category | flops | bytes accessed | tf_op | source)
XLA Modules:
  0.0 1187.9 jit_solution(7275630329626975454)
XLA Ops:
  10.7 6.2 gather_fusion.1
  20.8 96.5 %all-reduce.8.cloned.1.call-done = (f32[512,1024]{1,0:T(8,128)}, f32[128,512]{0,1:T(8,128)}) async-done(((f32[512,1024]{1,0:T(8,128)}, f32[128,512]{0,1:T(8,128)}), (f32[512,1024]{1,0:T(8,128)}, f32[128,512]{0,1:T(8,128)})) %all-reduce.8.cloned.1.call-update) | async-done | bytes 2359312 | tf_op jit(solution)/shard_map/psum | solution.py:35
  122.5 118.5 %all-reduce.6.cloned.1.call-done = f32[512,512]{1,0:T(8,128)} async-done(((f32[512,512]{1,0:T(8,128)}), f32[512,512]{1,0:T(8,128)}) %all-reduce.6.cloned.1.call-update) | async-done | bytes 1048592 | tf_op jit(solution)/shard_map/psum | solution.py:37
  246.9 45.8 %all-gather.13.cloned.1.call-done = f32[512,512]{0,1:T(8,128)} async-done(((f32[512,64]{0,1:T(8,128)}), f32[512,512]{0,1:T(8,128)}) %all-gather.13.cloned.1.call-update) | async-done | bytes 1048592 | tf_op jit(solution)/shard_map/all_gather | solution.py:60
  297.5 44.0 %all-gather.15.cloned.1.call-done = f32[512,512]{0,1:T(8,128)} async-done(((f32[512,64]{0,1:T(8,128)}), f32[512,512]{0,1:T(8,128)}) %all-gather.15.cloned.1.call-update) | async-done | bytes 1048592 | tf_op jit(solution)/shard_map/all_gather | solution.py:60
  341.5 2.7 fusion.9
  346.3 44.0 %all-gather.17.cloned.1.call-done = f32[512,512]{0,1:T(8,128)} async-done(((f32[512,64]{0,1:T(8,128)}), f32[512,512]{0,1:T(8,128)}) %all-gather.17.cloned.1.call-update) | async-done | bytes 1048592 | tf_op jit(solution)/shard_map/all_gather | solution.py:60
  395.1 44.0 %all-gather.19.cloned.1.call-done = f32[512,512]{0,1:T(8,128)} async-done(((f32[512,64]{0,1:T(8,128)}), f32[512,512]{0,1:T(8,128)}) %all-gather.19.cloned.1.call-update) | async-done | bytes 1048592 | tf_op jit(solution)/shard_map/all_gather | solution.py:60
  443.9 44.1 %all-gather.21.cloned.1.call-done = f32[512,512]{0,1:T(8,128)} async-done(((f32[512,64]{0,1:T(8,128)}), f32[512,512]{0,1:T(8,128)}) %all-gather.21.cloned.1.call-update) | async-done | bytes 1048592 | tf_op jit(solution)/shard_map/all_gather | solution.py:60
  493.1 43.8 %all-gather.23.cloned.1.call-done = f32[512,512]{0,1:T(8,128)} async-done(((f32[512,64]{0,1:T(8,128)}), f32[512,512]{0,1:T(8,128)}) %all-gather.23.cloned.1.call-update) | async-done | bytes 1048592 | tf_op jit(solution)/shard_map/all_gather | solution.py:60
  541.6 44.1 %all-gather.25.cloned.1.call-done = f32[512,512]{0,1:T(8,128)} async-done(((f32[512,64]{0,1:T(8,128)}), f32[512,512]{0,1:T(8,128)}) %all-gather.25.cloned.1.call-update) | async-done | bytes 1048592 | tf_op jit(solution)/shard_map/all_gather | solution.py:60
  585.7 2.7 fusion.14
  590.5 44.0 %all-gather.27.cloned.1.call-done = f32[512,512]{0,1:T(8,128)} async-done(((f32[512,64]{0,1:T(8,128)}), f32[512,512]{0,1:T(8,128)}) %all-gather.27.cloned.1.call-update) | async-done | bytes 1048592 | tf_op jit(solution)/shard_map/all_gather | solution.py:60
  638.9 9.2 copy.17
  648.0 8.8 gather_fusion
  656.8 4.7 fusion
  661.5 5.4 copy.18
  668.2 15.2 %all-gather.29.cloned.1.call-done = f32[512,512]{0,1:T(8,128)} async-done(((f32[512,64]{0,1:T(8,128)}), f32[512,512]{0,1:T(8,128)}) %all-gather.29.cloned.1.call-update) | async-done | bytes 1048592 | tf_op jit(solution)/shard_map/all_gather | solution.py:63
  686.0 123.5 %all-reduce.10.cloned.1.call-done = (bf16[512,1024]{1,0:T(8,128)(2,1)}, bf16[512,1024]{1,0:T(8,128)(2,1)}) async-done(((bf16[512,1024]{1,0:T(8,128)(2,1)}, bf16[512,1024]{1,0:T(8,128)(2,1)}), (bf16[512,1024]{1,0:T(8,128)(2,1)}, bf16[512,1024]{1,0:T(8,128)(2,1)})) %all-reduce.10.cloned.1.call-update) | async-done | bytes 2097168 | tf_op jit(solution)/shard_map/psum | solution.py:11
  809.5 2.9 fusion.2
  812.4 4.8 fusion.16
  817.2 323.2 %all-gather.11.cloned.1.call-done = f32[16,2048,512]{2,1,0:T(8,128)} async-done(((f32[1,2048,512]{2,1,0:T(8,128)}), f32[16,2048,512]{2,1,0:T(8,128)}) %all-gather.11.cloned.1.call-update) | async-done | bytes 67108880 | tf_op jit(solution)/shard_map/all_gather | solution.py:40
  1140.4 23.1 %reduce_sum.18 = f32[2048,512]{1,0:T(8,128)} reduce(f32[16,2048,512]{2,1,0:T(8,128)} %all-gather.11.cloned.1.call-done, f32[]{:T(128)} %constant.45.clone.1), dimensions={0}, to_apply=%region_0.1 | reduce | flops 15728640 | bytes 71303168
  1163.5 17.8 %convolution_subtract_fusion = f32[2048,1024]{1,0:T(8,128)} fusion(f32[2048,1024]{1,0:T(8,128)} %param.3, f32[2048,512]{1,0:T(8,128)} %reduce_sum.18, f32[512,1024]{1,0:T(8,128)S(1)} %copy-done.2), kind=kOutput, calls=%fused_computation.7 | convolution fusion | flops 12886999040 | bytes 23068672 | tf_op jit(solution)/shard_map/dot_general | solution.py:69
  (73 shorter events, 54.3 us)
Async XLA Ops:
  7.2 110.2 %all-reduce.8.cloned.1.call-start = ((), (), s32[]{:S(2)}) async-start(), calls=%async_computation.11 | async-start | bytes 4718592 | tf_op jit(solution)/shard_map/psum | solution.py:35
  20.7 220.2 %all-reduce.6.cloned.1.call-start = ((), (), s32[]{:S(2)}) async-start(), calls=%async_computation.1 | async-start | bytes 2097152 | tf_op jit(solution)/shard_map/psum | solution.py:37
  122.4 170.4 %all-gather.13.cloned.1.call-start = ((), (), s32[]{:S(2)}) async-start(), calls=%async_computation.2 | async-start | bytes 1179648 | tf_op jit(solution)/shard_map/all_gather | solution.py:60
  241.0 54.5 %copy-start = (f32[512,512]{1,0:T(8,128)S(1)}, f32[512,512]{1,0:T(8,128)}, u32[]{:S(2)}) copy-start(f32[512,512]{1,0:T(8,128)} %all-reduce.6.cloned.1.call-done) | copy-start | bytes 3145732
  244.5 97.0 %all-gather.15.cloned.1.call-start = ((), (), s32[]{:S(2)}) async-start(), calls=%async_computation.3 | async-start | bytes 1179648 | tf_op jit(solution)/shard_map/all_gather | solution.py:60
  295.4 94.9 %all-gather.17.cloned.1.call-start = ((), (), s32[]{:S(2)}) async-start(), calls=%async_computation.4 | async-start | bytes 1179648 | tf_op jit(solution)/shard_map/all_gather | solution.py:60
  344.2 94.9 %all-gather.19.cloned.1.call-start = ((), (), s32[]{:S(2)}) async-start(), calls=%async_computation.5 | async-start | bytes 1179648 | tf_op jit(solution)/shard_map/all_gather | solution.py:60
  393.0 95.0 %all-gather.21.cloned.1.call-start = ((), (), s32[]{:S(2)}) async-start(), calls=%async_computation.6 | async-start | bytes 1179648 | tf_op jit(solution)/shard_map/all_gather | solution.py:60
  441.8 95.1 %all-gather.23.cloned.1.call-start = ((), (), s32[]{:S(2)}) async-start(), calls=%async_computation.7 | async-start | bytes 1179648 | tf_op jit(solution)/shard_map/all_gather | solution.py:60
  490.6 146.6 %copy-start.1 = (f32[512,1024]{1,0:T(8,128)S(1)}, f32[512,1024]{1,0:T(8,128)}, u32[]{:S(2)}) copy-start(f32[512,1024]{1,0:T(8,128)} %get-tuple-element.4) | copy-start | bytes 6291460
  490.6 95.1 %all-gather.25.cloned.1.call-start = ((), (), s32[]{:S(2)}) async-start(), calls=%async_computation.8 | async-start | bytes 1179648 | tf_op jit(solution)/shard_map/all_gather | solution.py:60
  539.5 95.0 %all-gather.27.cloned.1.call-start = ((), (), s32[]{:S(2)}) async-start(), calls=%async_computation.9 | async-start | bytes 1179648 | tf_op jit(solution)/shard_map/all_gather | solution.py:60
  588.4 95.0 %all-gather.29.cloned.1.call-start = ((), (), s32[]{:S(2)}) async-start(), calls=%async_computation.10 | async-start | bytes 1179648 | tf_op jit(solution)/shard_map/all_gather | solution.py:63
  637.2 172.3 %all-reduce.10.cloned.1.call-start = ((), (), s32[]{:S(2)}) async-start(), calls=%async_computation.12 | async-start | bytes 4194304 | tf_op jit(solution)/shard_map/psum | solution.py:11
  638.8 501.6 %all-gather.11.cloned.1.call-start = ((), (), s32[]{:S(2)}) async-start(), calls=%async_computation | async-start | bytes 71303168 | tf_op jit(solution)/shard_map/all_gather | solution.py:40
  666.9 0.7 copy-start.5
  666.9 16.5 %copy-start.4 = (f32[128,512]{0,1:T(8,128)S(1)}, f32[128,512]{0,1:T(8,128)}, u32[]{:S(2)}) copy-start(f32[128,512]{0,1:T(8,128)} %get-tuple-element.5) | copy-start | bytes 786436
  683.4 129.0 %copy-start.3 = (f32[512,512]{0,1:T(8,128)S(1)}, f32[512,512]{0,1:T(8,128)}, u32[]{:S(2)}) copy-start(f32[512,512]{0,1:T(8,128)} %all-gather.29.cloned.1.call-done) | copy-start | bytes 3145732
  817.2 346.4 %copy-start.2 = (f32[512,1024]{1,0:T(8,128)S(1)}, f32[512,1024]{1,0:T(8,128)}, u32[]{:S(2)}) copy-start(f32[512,1024]{1,0:T(8,128)} %fusion.16) | copy-start | bytes 6291460
Sparse Core Ops, SparseCore 0:
  20.9 96.4 all-reduce.7
  122.5 118.4 all-reduce.5
  244.6 48.0 all-gather.12
  295.5 45.9 all-gather.14
  344.3 45.9 all-gather.16
  393.1 45.9 all-gather.18
  442.0 45.9 all-gather.20
  490.9 45.9 all-gather.22
  539.7 45.9 all-gather.24
  588.5 45.9 all-gather.26
  637.4 45.9 all-gather.28
  685.8 123.6 all-reduce.9
  811.2 329.1 all-gather.10
